TPU v7x, 32 devices: a whole 2x2x4 slice. The times are simulated.
32 devices in a mesh: seq: 16 (over z, y, x), head: 2 (over core).
Axes of the slice: x: 2, y: 2, z: 4, core: 2. Of those that a mesh axis runs over, the one named last changes fastest.
Arguments:
- x_inner: bfloat16 [2, 8192, 5120], P(None, 'seq', 'head'), may hold values from -6 to 6
- z_gate: bfloat16 [2, 8192, 5120], P(None, 'seq', 'head'), may hold values from -200 to 200
- b_input: bfloat16 [2, 8192, 128], P(None, 'seq'), may hold values from -6 to 6
- c_output: bfloat16 [2, 8192, 128], P(None, 'seq'), may hold values from -6 to 6
- step_sizes: float32 [2, 8192, 80], P(None, 'seq', 'head'), may hold values from 0.0002 to 0.2
- decay_log: float32 [80], P('head'), may hold values from -20 to 2
- skip_gain: float32 [80], P('head'), may hold values from 1 to 4
- norm_gain: float32 [5120], P('head'), may hold values from 0.5 to 1.5
- goal_pos: int32 [2, 512], P(None, 'seq'), may hold values from 0 to 8191, as said below
- goal_owner: int32 [2, 512], P(None, 'seq'), may hold values from 0 to 15, as said below
- value_w1: bfloat16 [16, 5120, 1024], P('seq', None, 'head'), may hold values from -0.078125 to 0.078125
- value_b1: float32 [16, 1024], P('seq', 'head'), may hold values from -3 to 3
- value_w2: bfloat16 [16, 1024], P('seq', 'head'), may hold values from -0.1875 to 0.1875
Outputs:
- layer_out: bfloat16 [2, 8192, 5120], P(None, 'seq', 'head')
- values: float32 [2, 512], P(None, 'seq')
Inputs may be any that keep to these rules, and one draw needn't show every extreme that they name: For every sequence s and every b, goal_pos[s, b * 32 + i] for i < 32 are distinct positions from b * 512 to (b + 1) * 512 - 1, increasing in i. `goal_owner`: among the 2 x 32 goals of the columns b * 32 to (b + 1) * 32 - 1, no expert is named more than 4 times; one expert is named exactly 4 times in every such group of columns.
All inputs are finite; a program needn't handle non-finite values.
Results may differ from a plain program's by a relative error of at most 0.0056.
Values may be sent and summed in bfloat16 or wider, within the bound.
No kernel may reach another device: no remote copies, remote signals or barrier semaphores. Data moves between devices by JAX's collectives and lax.ppermute only.
A program may use at most 384 MiB of HBM per device.

v0:
```python
import jax
import jax.numpy as jnp
from jax import lax
from jax.sharding import PartitionSpec as P

HEAD_TOTAL = 80
HEAD_DIM = 64
BLOCK = 256
CAP = 4
norm_eps = 1e-05


def carried_in(value, axis, combine, identity):
    length, index = (lax.axis_size(axis), lax.axis_index(axis))
    everything = jax.tree.map(lambda part: lax.all_gather(part, axis), value)
    start = jax.tree.map(
        lambda part, zero: jnp.broadcast_to(jnp.asarray(zero, part.dtype), part.shape),
        value,
        identity,
    )

    def hop(k, before):
        reached = k < index
        new = combine(before, jax.tree.map(lambda part: part[k], everything))
        return jax.tree.map(lambda a, b: jnp.where(reached, a, b), new, before)

    return lax.fori_loop(0, length, hop, start)


def block_parts(x_seq, b_seq, c_seq, dt_seq, decay_rates):
    length = x_seq.shape[0]
    head_count = dt_seq.shape[1]
    block_count = length // BLOCK
    x_blocks = x_seq.reshape(block_count, BLOCK, head_count, -1)
    b_blocks = b_seq.reshape(block_count, BLOCK, -1)
    c_blocks = c_seq.reshape(block_count, BLOCK, -1)
    dt_blocks = jnp.transpose(dt_seq.reshape(block_count, BLOCK, head_count), (0, 2, 1))
    cumulative = jnp.cumsum(dt_blocks * decay_rates[None, :, None], axis=2)
    end_weights = jnp.exp(cumulative[:, :, -1:] - cumulative) * dt_blocks
    x_weighted = (x_blocks * jnp.transpose(end_weights, (0, 2, 1))[..., None]).astype(jnp.bfloat16)
    states = jnp.einsum("crhp,crn->chpn", x_weighted, b_blocks, preferred_element_type=jnp.float32)
    return (x_blocks, b_blocks, c_blocks, dt_blocks, cumulative, states)


def diagonal_part(x_blocks, b_blocks, c_blocks, dt_blocks, cumulative):
    routing_scores = jnp.einsum(
        "ckn,crn->ckr", c_blocks, b_blocks, preferred_element_type=jnp.float32
    )
    positions = jnp.arange(BLOCK)
    lower_mask = positions[:, None] >= positions[None, :]
    spread = cumulative[:, :, :, None] - cumulative[:, :, None, :]
    decay_mat = jnp.exp(jnp.where(lower_mask, spread, -jnp.inf))
    weights = (routing_scores[:, None] * decay_mat * dt_blocks[:, :, None, :]).astype(jnp.bfloat16)
    return jnp.einsum("chkr,crhp->ckhp", weights, x_blocks, preferred_element_type=jnp.float32)


def chain_combine(earlier, later):
    return (earlier[0] + later[0], jnp.exp(later[0])[..., None, None] * earlier[1] + later[1])


def pick_rows(layer_seq, index_seq):
    return jnp.take(layer_seq, index_seq, axis=0)


def value_terms(full_rows, value_w1, value_b1, value_w2):
    hidden = (
        jnp.einsum("sjw,wv->sjv", full_rows, value_w1[0], preferred_element_type=jnp.float32)
        + value_b1[0]
    )
    hidden = jax.nn.gelu(hidden).astype(jnp.bfloat16)
    return jnp.einsum("sjv,v->sj", hidden, value_w2[0], preferred_element_type=jnp.float32)


def finish_values(partial_sum):
    partial_sum = lax.psum(partial_sum, "head")
    return lax.all_to_all(partial_sum, "seq", split_axis=0, concat_axis=0, tiled=True)


def body(
    x_inner,
    z_gate,
    b_input,
    c_output,
    step_sizes,
    decay_log,
    skip_gain,
    norm_gain,
    goal_pos,
    goal_owner,
    value_w1,
    value_b1,
    value_w2,
):
    decay_rates = -jnp.exp(decay_log)
    seq_count = x_inner.shape[0]
    length = x_inner.shape[1]
    stored = []
    decay_sums = []
    state_sums = []
    for seq_index in range(seq_count):
        pieces = block_parts(
            x_inner[seq_index],
            b_input[seq_index],
            c_output[seq_index],
            step_sizes[seq_index],
            decay_rates,
        )
        totals = pieces[4][:, :, -1]
        entering = [jnp.zeros_like(pieces[5][0])]
        for block_index in range(totals.shape[0]):
            entering.append(
                jnp.exp(totals[block_index])[:, None, None] * entering[-1] + pieces[5][block_index]
            )
        stored.append((pieces, totals, entering))
        decay_sums.append(jnp.sum(totals, axis=0))
        state_sums.append(entering[-1])
    summary = (jnp.stack(decay_sums), jnp.stack(state_sums))
    identity = (jnp.zeros_like(summary[0]), jnp.zeros_like(summary[1]))
    incoming = carried_in(summary, "seq", chain_combine, identity)[1]
    outputs = []
    for seq_index in range(seq_count):
        pieces, totals, entering = stored[seq_index]
        x_blocks, b_blocks, c_blocks, dt_blocks, cumulative, states = pieces
        y_diag = diagonal_part(x_blocks, b_blocks, c_blocks, dt_blocks, cumulative)
        prior = jnp.cumsum(totals, axis=0) - totals
        carried = (
            jnp.exp(prior)[:, :, None, None] * incoming[seq_index][None] + jnp.stack(entering[:-1])
        ).astype(jnp.bfloat16)
        y_off = (
            jnp.einsum("ckn,chpn->ckhp", c_blocks, carried, preferred_element_type=jnp.float32)
            * jnp.exp(jnp.transpose(cumulative, (0, 2, 1)))[..., None]
        )
        y_all = y_diag + y_off + skip_gain[None, None, :, None] * x_blocks
        outputs.append(y_all.reshape(length, -1))
    y_full = jnp.stack(outputs)
    gated_out = y_full * jax.nn.silu(z_gate.astype(jnp.float32))
    squares = lax.psum(jnp.sum(gated_out * gated_out, axis=-1), "head")
    inv_rms = lax.rsqrt(squares / (HEAD_TOTAL * HEAD_DIM) + norm_eps)
    layer_out = (gated_out * inv_rms[..., None] * norm_gain).astype(jnp.bfloat16)
    goal_dev = goal_pos.shape[1]
    local_pos = goal_pos - lax.axis_index("seq") * length
    picked_rows = jax.vmap(pick_rows)(layer_out, local_pos).reshape(seq_count * goal_dev, -1)
    owners = goal_owner.reshape(-1)
    row_ids = jnp.arange(owners.shape[0])
    same_owner = (owners[:, None] == owners[None, :]) & (row_ids[None, :] < row_ids[:, None])
    slot_rank = jnp.sum(same_owner.astype(jnp.int32), axis=1)
    slot_index = owners * CAP + slot_rank
    experts = lax.axis_size("seq")
    slot_numbers = jnp.arange(experts * CAP)
    placing = (slot_numbers[:, None] == slot_index[None, :]).astype(jnp.bfloat16)
    whole_rows = lax.all_gather(picked_rows, "head", axis=1, tiled=True)
    routed_full = (
        jnp.dot(placing, whole_rows, preferred_element_type=jnp.float32)
        .astype(jnp.bfloat16)
        .reshape(experts, CAP, -1)
    )
    returned = finish_values(
        value_terms(
            lax.all_to_all(routed_full, "seq", split_axis=0, concat_axis=0, tiled=True),
            value_w1,
            value_b1,
            value_w2,
        )
    )
    picked = jnp.take(returned.reshape(-1), slot_index)
    values = picked.reshape(seq_count, goal_dev)
    return (layer_out, values)


def solution(mesh):
    placed = (
        P(None, "seq", "head"),
        P(None, "seq", "head"),
        P(None, "seq", None),
        P(None, "seq", None),
        P(None, "seq", "head"),
        P("head"),
        P("head"),
        P("head"),
        P(None, "seq"),
        P(None, "seq"),
        P("seq", None, "head"),
        P("seq", "head"),
        P("seq", "head"),
    )
    return jax.shard_map(
        body,
        mesh=mesh,
        in_specs=placed,
        out_specs=(P(None, "seq", "head"), P(None, "seq")),
        check_vma=False,
    )
```

profile of v0, /device:TPU:0, one launch (start us, length us, event | category | flops | bytes accessed | tf_op | source)
XLA Modules:
  0.0 669.2 jit_solution(8477946099829321307)
XLA Ops:
  15.7 4.4 fusion.94
  20.0 7.5 %reshape.263 = bf16[2,256,40,64]{3,2,1,0:T(8,128)(2,1)} reshape(bf16[1,512,2560]{2,1,0:T(8,128)(2,1)} %get-tuple-element.139) | data formatting | bytes 5242880 | tf_op jit(solution)/shard_map/reshape;squeeze | solution.py:34
  27.6 6.4 copy.99
  35.2 4.4 reshape.264
  39.6 5.2 copy.107
  44.8 3.5 fusion.29
  57.8 44.9 %all-gather.2 = f32[16,2,40]{2,1,0:T(2,128)} all-gather(f32[1,2,40]{2,1,0:T(2,128)S(1)} %maximum_bitcast_fusion), channel_id=2, replica_groups=mesh['seq'=16,'head'=2] {'seq'}, dimensions={0}, use_global_device_ids=true | all-gather | bytes 5440 | tf_op jit(solution)/shard_map/all_gather | solution.py:15
  110.6 375.5 %all-gather.5.cloned.1.call-done = f32[32,40,64,128]{3,2,1,0:T(8,128)} async-done(((f32[2,40,64,128]{3,2,1,0:T(8,128)}), f32[32,40,64,128]{3,2,1,0:T(8,128)}) %all-gather.5.cloned.1.call-update) | async-done | bytes 41943056 | tf_op jit(solution)/shard_map/all_gather | solution.py:15
  486.1 48.5 %while.14 = (s32[]{:T(128)}, f32[2,40,64,128]{3,2,1,0:T(8,128)S(1)}, s32[]{:T(128)}, f32[16,2,40]{2,1,0:T(2,128)}, f32[16,2,40,64,128]{4,3,2,1,0:T(8,128)}, /*index=5*/s32[]{:T(128)}, s32[]{:T(128)}) while((s32[]{:T(128)}, f32[2,40,64,128]{3,2,1,0:T(8,128)S(1)}, s32[]{:T(128)}, f32[16,2,40]{2,1,0:T(2,128)}, ...), condition=%wide.region_8.9_spmd.clone, body=%wide.region_7.8_spmd.clone.sunk | while | flops 2621444 | bytes 7865385 | solution.py:27
  537.8 7.9 %fusion.20 = f32[2,256,40,64]{1,3,2,0:T(8,128)} fusion(bf16[2,256,40,64]{1,3,2,0:T(8,128)(2,1)S(1)} %copy-done.4, f32[2,40,64,256]{3,2,1,0:T(8,128)S(1)} %fusion.33, f32[40]{0:T(128)S(1)} %copy-done.25, f32[2,256,40]{1,2,0:T(8,128)S(1)} %copy-done.10, f32[2,40,256]{2,1,0:T(8,128)S(1)} %copy.97, f32[2,40,256]{2,1,0:T(8,128)S(1)} %copy_bitcast_fusion.1, ...), kind=kOutput, calls=%fused_computation.35 | convolution fusion | flops 703856640 | bytes 13942944 | tf_op jit(solution)/shard_map/chkr,crhp->ckhp/dot_general | solution.py:54
  545.7 8.6 %copy.124 = f32[2,256,40,64]{3,2,1,0:T(8,128)} copy(f32[2,256,40,64]{1,3,2,0:T(8,128)} %fusion.20) | data formatting | bytes 10485760 | tf_op jit(solution)/shard_map/stack;reshape | solution.py:135
  554.4 9.7 %reshape.260 = f32[1,512,2560]{2,1,0:T(8,128)} reshape(f32[2,256,40,64]{3,2,1,0:T(8,128)} %copy.124) | data formatting | bytes 10485760 | tf_op jit(solution)/shard_map/stack;reshape | solution.py:135
  566.0 7.9 %fusion.22 = f32[2,256,40,64]{1,3,2,0:T(8,128)} fusion(bf16[2,256,40,64]{1,3,2,0:T(8,128)(2,1)S(1)} %copy-done.3, f32[2,40,64,256]{3,2,1,0:T(8,128)S(1)} %fusion.34, f32[2,256,40]{1,2,0:T(8,128)S(1)} %copy-done.9, f32[40]{0:T(128)S(1)} %copy-done.25, f32[2,40,256]{2,1,0:T(8,128)S(1)} %copy.112, f32[2,40,256]{2,1,0:T(8,128)S(1)} %copy_bitcast_fusion, ...), kind=kOutput, calls=%fused_computation.37 | convolution fusion | flops 703856640 | bytes 13942944 | tf_op jit(solution)/shard_map/chkr,crhp->ckhp/dot_general | solution.py:54
  573.9 8.6 %copy.125 = f32[2,256,40,64]{3,2,1,0:T(8,128)} copy(f32[2,256,40,64]{1,3,2,0:T(8,128)} %fusion.22) | data formatting | bytes 10485760 | tf_op jit(solution)/shard_map/stack;reshape | solution.py:135
  582.5 9.6 %reshape.261 = f32[1,512,2560]{2,1,0:T(8,128)} reshape(f32[2,256,40,64]{3,2,1,0:T(8,128)} %copy.125) | data formatting | bytes 10485760 | tf_op jit(solution)/shard_map/stack;reshape | solution.py:135
  592.1 11.9 %multiply_reduce_fusion = (f32[2,512]{1,0:T(2,128)S(1)}, f32[2,512,2560]{2,1,0:T(8,128)}) fusion(bf16[2,512,2560]{2,1,0:T(8,128)(2,1)} %param.16, f32[1,512,2560]{2,1,0:T(8,128)} %reshape.261, f32[1,512,2560]{2,1,0:T(8,128)} %reshape.260), kind=kLoop, calls=%fused_computation.16 | loop fusion | flops 23591936 | bytes 26218496 | tf_op jit(solution)/shard_map/reduce_sum | solution.py:137
  604.0 2.4 psum.14
  606.4 7.3 %multiply_convert_fusion.4 = bf16[2,512,2560]{2,1,0:T(8,128)(2,1)} fusion(f32[2,512,2560]{2,1,0:T(8,128)} %get-tuple-element.134, f32[2560]{0:T(1024)S(1)} %copy-done.15, f32[2,512]{1,0:T(2,128)S(1)} %add_rsqrt_fusion), kind=kLoop, calls=%fused_computation.15 | loop fusion | flops 7864320 | bytes 15742976 | tf_op jit(solution)/shard_map/convert_element_type | solution.py:139
  619.7 3.8 all-to-all-start
  623.6 17.6 %all-to-all-done = bf16[16,4,5120]{2,1,0:T(4,128)(2,1)S(1)} async-done(((bf16[16,4,5120]{2,1,0:T(4,128)(2,1)}), bf16[16,4,5120]{2,1,0:T(4,128)(2,1)S(1)}, u32[]{:S(2)}, u32[]{:S(2)}) %all-to-all-start) | async-done | bytes 655392 | tf_op jit(solution)/shard_map/all_to_all | solution.py:159
  641.2 3.6 fusion.61
  644.8 2.5 psum.15
  647.9 4.4 all-to-all-start.1
  652.5 7.2 %all-to-all-done.1 = f32[16,1,4]{2,1,0:T(1,128)S(1)} async-done(((f32[16,1,4]{2,1,0:T(1,128)}), f32[16,1,4]{2,1,0:T(1,128)S(1)}, u32[]{:S(2)}, u32[]{:S(2)}) %all-to-all-start.1) | async-done | bytes 288 | tf_op jit(solution)/shard_map/all_to_all | solution.py:76
  (165 shorter events, 89.5 us)
Async XLA Ops:
  7.2 634.1 %copy-start = (bf16[1,512]{1,0:T(2,128)(2,1)S(1)}, bf16[1,512]{1,0:T(2,128)(2,1)}, u32[]{:S(2)}) copy-start(bf16[1,512]{1,0:T(2,128)(2,1)} %param.27) | copy-start | bytes 3076
  7.2 478.9 %all-gather.5.cloned.1.call-start = ((), (), s32[]{:S(2)}) async-start(), calls=%async_computation.2 | async-start | bytes 44564480 | tf_op jit(solution)/shard_map/all_gather | solution.py:15
  14.6 20.3 %copy-start.13 = (f32[2,40]{1,0:T(2,128)}, f32[2,40]{1,0:T(2,128)S(1)}, u32[]{:S(2)}) copy-start(f32[2,40]{1,0:T(2,128)S(1)} %get-tuple-element.122) | copy-start | bytes 964
  44.8 4.4 copy-start.2
  44.8 4.4 copy-start.19
  44.8 4.4 copy-start.20
  44.8 4.4 copy-start.21
  44.8 4.4 copy-start.22
  51.2 2.5 copy-start.14
  102.9 3.9 copy-start.26
  535.9 1.9 copy-start.8
  535.9 1.9 copy-start.10
  535.9 1.9 copy-start.11
  535.9 1.9 copy-start.25
  554.4 9.8 %copy-start.1 = (f32[40,64,128]{2,1,0:T(8,128)S(1)}, f32[40,64,128]{2,1,0:T(8,128)}, u32[]{:S(2)}) copy-start(f32[40,64,128]{2,1,0:T(8,128)} %get-tuple-element.142) | copy-start | bytes 3932164
  554.4 9.8 %copy-start.5 = (f32[1,40,64,128]{3,2,1,0:T(8,128)S(1)}, f32[1,40,64,128]{3,2,1,0:T(8,128)}, u32[]{:S(2)}) copy-start(f32[1,40,64,128]{3,2,1,0:T(8,128)} %get-tuple-element.138) | copy-start | bytes 3932164
  592.1 14.4 %copy-start.15 = (f32[2560]{0:T(1024)S(1)}, f32[2560]{0:T(1024)}, u32[]{:S(2)}) copy-start(f32[2560]{0:T(1024)} %param.22) | copy-start | bytes 30724
  606.4 9.5 %copy-start.24 = (pred[64]{0:T(512)(128)(4,1)S(1)}, pred[64]{0:T(512)(128)(4,1)}, u32[]{:S(2)}) copy-start(pred[64]{0:T(512)(128)(4,1)} %broadcast_in_dim.35) | copy-start | bytes 196
  606.4 11.9 %copy-start.23 = (s32[64]{0:T(128)S(1)}, s32[64]{0:T(128)}, u32[]{:S(2)}) copy-start(s32[64]{0:T(128)} %multiply_add_fusion) | copy-start | bytes 772
  613.7 9.8 %copy-start.17 = (s32[2,32]{1,0:T(2,128)S(1)}, s32[2,32]{1,0:T(2,128)}, u32[]{:S(2)}) copy-start(s32[2,32]{1,0:T(2,128)} %param.24) | copy-start | bytes 772
  613.7 9.9 %copy-start.27 = (s32[64]{0:T(128)S(1)}, s32[64]{0:T(128)}, u32[]{:S(2)}) copy-start(s32[64]{0:T(128)} %copy-done.26) | copy-start | bytes 772
  613.7 27.5 %copy-start.18 = (f32[1,512]{1,0:T(1,128)S(1)}, f32[1,512]{1,0:T(1,128)}, u32[]{:S(2)}) copy-start(f32[1,512]{1,0:T(1,128)} %param.26) | copy-start | bytes 6148
  619.7 21.5 %all-to-all-start = ((bf16[16,4,5120]{2,1,0:T(4,128)(2,1)}), bf16[16,4,5120]{2,1,0:T(4,128)(2,1)S(1)}, u32[]{:S(2)}, u32[]{:S(2)}) async-start(bf16[16,4,5120]{2,1,0:T(4,128)(2,1)} %reshape.226), calls=%async_computation | async-start | bytes 1310720 | tf_op jit(solution)/shard_map/all_to_all | solution.py:159
  647.9 11.7 %all-to-all-start.1 = ((f32[16,1,4]{2,1,0:T(1,128)}), f32[16,1,4]{2,1,0:T(1,128)S(1)}, u32[]{:S(2)}, u32[]{:S(2)}) async-start(f32[16,1,4]{2,1,0:T(1,128)} %copy.118), calls=%async_computation.1 | async-start | bytes 16384 | tf_op jit(solution)/shard_map/all_to_all | solution.py:76
  (7 other events, 12.2 us)
Sparse Core Ops, SparseCore 0:
  53.2 432.8 all-gather.4
where the time goes:
time: 672 us; the launch traced here: 669 us
  waiting for transfers between devices  400 us (60%)
  local copies, waits for them, and re-layouts  89 us (13%)
  other arithmetic  76.8 us (11%)
  blocking collectives  52.1 us (8%)
  matrix products  27.9 us (4%)
  between operations  14.5 us (2%)
  starting transfers between devices  8.28 us (1%)
    all_gather x1, waiting for transfers between devices, carried_in(): everything = jax.tree.map(lambda part: lax.all_gather(part, axis), value)  375 us
    all_gather x1, blocking collectives, carried_in(): everything = jax.tree.map(lambda part: lax.all_gather(part, axis), value)  44.9 us
    select_n x16, other arithmetic, hop(): return jax.tree.map(lambda a, b: jnp.where(reached, a, b), new, before)  37.7 us
    another operation x4, local copies, waits for them, and re-layouts, body(): y_full = jnp.stack(outputs)  36.6 us
    another operation x4, local copies, waits for them, and re-layouts, block_parts(): x_blocks = x_seq.reshape(block_count, BLOCK, head_count, -1)  23.5 us
    all_to_all x1, waiting for transfers between devices, body(): lax.all_to_all(routed_full, 'seq', split_axis=0, concat_axis=0, tiled=True)  17.6 us
    dot_general x2, matrix products, diagonal_part(): jnp.einsum('chkr,crhp->ckhp', weights, x_blocks, preferred_element_type=j...  15.8 us
  transfers between devices with their start and end apart: 3, of which 3 were waited for; matrix products, arithmetic and copies ran while one was open for 2% of the time, Pallas kernels for 0%

commit v1 on v0

--- a/solution.py
+++ b/solution.py
@@ -91,6 +91,27 @@
     value_b1,
     value_w2,
 ):
+
+    def _deliver_runs(local):
+        mixed_arr = lax.axis_index("seq")
+        clean = lax.axis_size("seq")
+        oldest, q_next = (clean, mixed_arr)
+        all_values = list(local.shape)
+        passed = local.shape[0] // oldest
+        all_values[0] = passed
+        last = all_values[0]
+        all_values[0] = last * oldest
+        wide_out = jnp.zeros(all_values, local.dtype)
+        for s in range(oldest):
+            y_new = lax.dynamic_slice_in_dim(local, (q_next ^ s) * passed, passed, axis=0)
+            if s:
+                f_next = range(oldest)
+                right_arr = map(lambda to_i: (to_i, to_i ^ s), f_next)
+                upper = list(right_arr)
+                y_new = lax.ppermute(y_new, "seq", perm=upper)
+            wide_out = lax.dynamic_update_slice_in_dim(wide_out, y_new, (q_next ^ s) * last, axis=0)
+        return wide_out
+
     decay_rates = -jnp.exp(decay_log)
     seq_count = x_inner.shape[0]
     length = x_inner.shape[1]
@@ -154,14 +175,7 @@
         .astype(jnp.bfloat16)
         .reshape(experts, CAP, -1)
     )
-    returned = finish_values(
-        value_terms(
-            lax.all_to_all(routed_full, "seq", split_axis=0, concat_axis=0, tiled=True),
-            value_w1,
-            value_b1,
-            value_w2,
-        )
-    )
+    returned = finish_values(value_terms(_deliver_runs(routed_full), value_w1, value_b1, value_w2))
     picked = jnp.take(returned.reshape(-1), slot_index)
     values = picked.reshape(seq_count, goal_dev)
     return (layer_out, values)

time: 672 us -> 697 us (1.037)
  starting transfers between devices: 8.28 us -> 29.2 us
  local copies, waits for them, and re-layouts: 89 us -> 103 us
  waiting for transfers between devices: 400 us -> 390 us
    ppermute x0 -> x15, starting transfers between devices: none -> 24.5 us  [_deliver_runs(): y_new = lax.ppermute(y_new, 'seq', perm=upper)]
    all_to_all x1 -> x0, waiting for transfers between devices: 17.6 us -> none  [body(): lax.all_to_all(routed_full, 'seq', split_axis=0, concat_axis=0, tiled=True)]
    dynamic_update_slice x0 -> x16, local copies, waits for them, and re-layouts: none -> 13.5 us  [_deliver_runs(): lax.dynamic_update_slice_in_dim(wide_out, y_new, (q_next ^ s) * last, axi...]
    ppermute x0 -> x15, waiting for transfers between devices: none -> 7.06 us  [_deliver_runs(): y_new = lax.ppermute(y_new, 'seq', perm=upper)]
  transfers between devices with their start and end apart: 3 -> 17, of which waited for: 3 -> 6; matrix products, arithmetic and copies ran while one was open for 2% -> 4% of each run, Pallas kernels for 0% -> 0%
where the time goes in v1:
time: 697 us; the launch traced here: 694 us
  waiting for transfers between devices  390 us (56%)
  local copies, waits for them, and re-layouts  103 us (15%)
  other arithmetic  76.8 us (11%)
  blocking collectives  52.3 us (8%)
  starting transfers between devices  29.2 us (4%)
  matrix products  28 us (4%)
  between operations  14.8 us (2%)
    all_gather x1, waiting for transfers between devices, carried_in(): everything = jax.tree.map(lambda part: lax.all_gather(part, axis), value)  375 us
    all_gather x1, blocking collectives, carried_in(): everything = jax.tree.map(lambda part: lax.all_gather(part, axis), value)  44.9 us
    select_n x16, other arithmetic, hop(): return jax.tree.map(lambda a, b: jnp.where(reached, a, b), new, before)  37.7 us
    another operation x4, local copies, waits for them, and re-layouts, body(): y_full = jnp.stack(outputs)  36.6 us
    ppermute x15, starting transfers between devices, _deliver_runs(): y_new = lax.ppermute(y_new, 'seq', perm=upper)  24.5 us
    another operation x4, local copies, waits for them, and re-layouts, block_parts(): x_blocks = x_seq.reshape(block_count, BLOCK, head_count, -1)  23.5 us
    dot_general x2, matrix products, diagonal_part(): jnp.einsum('chkr,crhp->ckhp', weights, x_blocks, preferred_element_type=j...  15.8 us
  transfers between devices with their start and end apart: 17, of which 6 were waited for; matrix products, arithmetic and copies ran while one was open for 4% of the time, Pallas kernels for 0%

profile of v1, /device:TPU:0, one launch (start us, length us, event | category | flops | bytes accessed | tf_op | source)
XLA Modules:
  0.0 694.2 jit_solution(11729738638569959172)
XLA Ops:
  15.7 4.4 fusion.87
  20.0 7.5 %reshape.263 = bf16[2,256,40,64]{3,2,1,0:T(8,128)(2,1)} reshape(bf16[1,512,2560]{2,1,0:T(8,128)(2,1)} %get-tuple-element.139) | data formatting | bytes 5242880 | tf_op jit(solution)/shard_map/reshape;squeeze | solution.py:34
  27.6 6.4 copy.159
  35.2 4.4 reshape.264
  39.6 5.2 copy.167
  44.8 3.5 fusion.29
  57.8 44.9 %all-gather.2 = f32[16,2,40]{2,1,0:T(2,128)} all-gather(f32[1,2,40]{2,1,0:T(2,128)S(1)} %maximum_bitcast_fusion), channel_id=2, replica_groups=mesh['seq'=16,'head'=2] {'seq'}, dimensions={0}, use_global_device_ids=true | all-gather | bytes 5440 | tf_op jit(solution)/shard_map/all_gather | solution.py:15
  110.6 375.5 %all-gather.5.cloned.1.call-done = f32[32,40,64,128]{3,2,1,0:T(8,128)} async-done(((f32[2,40,64,128]{3,2,1,0:T(8,128)}), f32[32,40,64,128]{3,2,1,0:T(8,128)}) %all-gather.5.cloned.1.call-update) | async-done | bytes 41943056 | tf_op jit(solution)/shard_map/all_gather | solution.py:15
  486.1 48.5 %while.14 = (s32[]{:T(128)}, f32[2,40,64,128]{3,2,1,0:T(8,128)S(1)}, s32[]{:T(128)}, f32[16,2,40]{2,1,0:T(2,128)}, f32[16,2,40,64,128]{4,3,2,1,0:T(8,128)}, /*index=5*/s32[]{:T(128)}, s32[]{:T(128)}) while((s32[]{:T(128)}, f32[2,40,64,128]{3,2,1,0:T(8,128)S(1)}, s32[]{:T(128)}, f32[16,2,40]{2,1,0:T(2,128)}, ...), condition=%wide.region_8.9_spmd.clone, body=%wide.region_7.8_spmd.clone.sunk | while | flops 2621444 | bytes 7865385 | solution.py:27
  537.8 7.9 %fusion.20 = f32[2,256,40,64]{1,3,2,0:T(8,128)} fusion(bf16[2,256,40,64]{1,3,2,0:T(8,128)(2,1)S(1)} %copy-done.4, f32[2,40,64,256]{3,2,1,0:T(8,128)S(1)} %fusion.33, f32[40]{0:T(128)S(1)} %copy-done.25, f32[2,256,40]{1,2,0:T(8,128)S(1)} %copy-done.10, f32[2,40,256]{2,1,0:T(8,128)S(1)} %copy.157, f32[2,40,256]{2,1,0:T(8,128)S(1)} %copy_bitcast_fusion.1, ...), kind=kOutput, calls=%fused_computation.35 | convolution fusion | flops 703856640 | bytes 13942944 | tf_op jit(solution)/shard_map/chkr,crhp->ckhp/dot_general | solution.py:54
  545.7 8.6 %copy.199 = f32[2,256,40,64]{3,2,1,0:T(8,128)} copy(f32[2,256,40,64]{1,3,2,0:T(8,128)} %fusion.20) | data formatting | bytes 10485760 | tf_op jit(solution)/shard_map/stack;reshape | solution.py:156
  554.4 9.7 %reshape.260 = f32[1,512,2560]{2,1,0:T(8,128)} reshape(f32[2,256,40,64]{3,2,1,0:T(8,128)} %copy.199) | data formatting | bytes 10485760 | tf_op jit(solution)/shard_map/stack;reshape | solution.py:156
  566.0 7.9 %fusion.22 = f32[2,256,40,64]{1,3,2,0:T(8,128)} fusion(bf16[2,256,40,64]{1,3,2,0:T(8,128)(2,1)S(1)} %copy-done.3, f32[2,40,64,256]{3,2,1,0:T(8,128)S(1)} %fusion.34, f32[2,256,40]{1,2,0:T(8,128)S(1)} %copy-done.9, f32[40]{0:T(128)S(1)} %copy-done.25, f32[2,40,256]{2,1,0:T(8,128)S(1)} %copy.172, f32[2,40,256]{2,1,0:T(8,128)S(1)} %copy_bitcast_fusion, ...), kind=kOutput, calls=%fused_computation.37 | convolution fusion | flops 703856640 | bytes 13942944 | tf_op jit(solution)/shard_map/chkr,crhp->ckhp/dot_general | solution.py:54
  573.9 8.6 %copy.200 = f32[2,256,40,64]{3,2,1,0:T(8,128)} copy(f32[2,256,40,64]{1,3,2,0:T(8,128)} %fusion.22) | data formatting | bytes 10485760 | tf_op jit(solution)/shard_map/stack;reshape | solution.py:156
  582.5 9.6 %reshape.261 = f32[1,512,2560]{2,1,0:T(8,128)} reshape(f32[2,256,40,64]{3,2,1,0:T(8,128)} %copy.200) | data formatting | bytes 10485760 | tf_op jit(solution)/shard_map/stack;reshape | solution.py:156
  592.1 11.9 %multiply_reduce_fusion = (f32[2,512]{1,0:T(2,128)S(1)}, f32[2,512,2560]{2,1,0:T(8,128)}) fusion(bf16[2,512,2560]{2,1,0:T(8,128)(2,1)} %param.16, f32[1,512,2560]{2,1,0:T(8,128)} %reshape.261, f32[1,512,2560]{2,1,0:T(8,128)} %reshape.260), kind=kLoop, calls=%fused_computation.16 | loop fusion | flops 23591936 | bytes 26218496 | tf_op jit(solution)/shard_map/reduce_sum | solution.py:158
  606.4 7.3 %multiply_convert_fusion.4 = bf16[2,512,2560]{2,1,0:T(8,128)(2,1)} fusion(f32[2,512,2560]{2,1,0:T(8,128)} %get-tuple-element.134, f32[2560]{0:T(1024)S(1)} %copy-done.15, f32[2,512]{1,0:T(2,128)S(1)} %add_rsqrt_fusion), kind=kLoop, calls=%fused_computation.15 | loop fusion | flops 7864320 | bytes 15742976 | tf_op jit(solution)/shard_map/convert_element_type | solution.py:160
  616.0 2.5 all_gather.19
  623.5 3.0 collective-permute-start.4
  627.3 2.5 collective-permute-start.6
  639.4 5.2 collective-permute-done.7
  665.9 3.7 fusion.55
  672.8 4.6 all-to-all-start
  677.5 7.2 %all-to-all-done = f32[16,1,4]{2,1,0:T(1,128)S(1)} async-done(((f32[16,1,4]{2,1,0:T(1,128)}), f32[16,1,4]{2,1,0:T(1,128)S(1)}, u32[]{:S(2)}, u32[]{:S(2)}) %all-to-all-start) | async-done | bytes 288 | tf_op jit(solution)/shard_map/all_to_all | solution.py:76
  (227 shorter events, 127.0 us)
Async XLA Ops:
  7.2 658.8 %copy-start = (bf16[1,512]{1,0:T(2,128)(2,1)S(1)}, bf16[1,512]{1,0:T(2,128)(2,1)}, u32[]{:S(2)}) copy-start(bf16[1,512]{1,0:T(2,128)(2,1)} %param.27) | copy-start | bytes 3076
  7.2 478.9 %all-gather.5.cloned.1.call-start = ((), (), s32[]{:S(2)}) async-start(), calls=%async_computation.1 | async-start | bytes 44564480 | tf_op jit(solution)/shard_map/all_gather | solution.py:15
  14.6 20.3 %copy-start.13 = (f32[2,40]{1,0:T(2,128)}, f32[2,40]{1,0:T(2,128)S(1)}, u32[]{:S(2)}) copy-start(f32[2,40]{1,0:T(2,128)S(1)} %get-tuple-element.122) | copy-start | bytes 964
  592.1 14.4 %copy-start.15 = (f32[2560]{0:T(1024)S(1)}, f32[2560]{0:T(1024)}, u32[]{:S(2)}) copy-start(f32[2560]{0:T(1024)} %param.22) | copy-start | bytes 30724
  606.4 12.1 %copy-start.23 = (s32[64]{0:T(128)S(1)}, s32[64]{0:T(128)}, u32[]{:S(2)}) copy-start(s32[64]{0:T(128)} %multiply_add_fusion) | copy-start | bytes 772
  613.7 21.5 %copy-start.17 = (s32[2,32]{1,0:T(2,128)S(1)}, s32[2,32]{1,0:T(2,128)}, u32[]{:S(2)}) copy-start(s32[2,32]{1,0:T(2,128)} %param.24) | copy-start | bytes 772
  613.7 38.4 %copy-start.27 = (s32[64]{0:T(128)S(1)}, s32[64]{0:T(128)}, u32[]{:S(2)}) copy-start(s32[64]{0:T(128)} %copy-done.26) | copy-start | bytes 772
  616.0 49.9 %copy-start.18 = (f32[1,512]{1,0:T(1,128)S(1)}, f32[1,512]{1,0:T(1,128)}, u32[]{:S(2)}) copy-start(f32[1,512]{1,0:T(1,128)} %param.26) | copy-start | bytes 6148
  619.5 7.4 %collective-permute-start = (bf16[1,4,5120]{2,0,1:T(2,128)(2,1)S(1)}, bf16[1,4,5120]{2,0,1:T(2,128)(2,1)S(1)}, u32[]{:S(2)}, u32[]{:S(2)}) collective-permute-start(bf16[1,4,5120]{2,0,1:T(2,128)(2,1)S(1)} %copy.208), channel_id=1, source_target_pairs={{0,2},{2,0},{4,6},{6,4},{8,10},{10,8},{12,14},{14,12},{16,18},{18,... | collective-permute-start | bytes 122888 | tf_op jit(solution)/shard_map/ppermute | solution.py:111
  621.1 6.3 collective-permute-start.1
  621.8 8.1 %collective-permute-start.2 = (bf16[1,4,5120]{2,0,1:T(2,128)(2,1)S(1)}, bf16[1,4,5120]{2,0,1:T(2,128)(2,1)S(1)}, u32[]{:S(2)}, u32[]{:S(2)}) collective-permute-start(bf16[1,4,5120]{2,0,1:T(2,128)(2,1)S(1)} %copy.210), channel_id=1, source_target_pairs={{0,6},{2,4},{4,2},{6,0},{8,14},{10,12},{12,10},{14,8},{16,22},{18,... | collective-permute-start | bytes 122888 | tf_op jit(solution)/shard_map/ppermute | solution.py:111
  623.4 8.0 %collective-permute-start.3 = (bf16[1,4,5120]{2,0,1:T(2,128)(2,1)S(1)}, bf16[1,4,5120]{2,0,1:T(2,128)(2,1)S(1)}, u32[]{:S(2)}, u32[]{:S(2)}) collective-permute-start(bf16[1,4,5120]{2,0,1:T(2,128)(2,1)S(1)} %copy.211), channel_id=1, source_target_pairs={{0,8},{2,10},{4,12},{6,14},{8,0},{10,2},{12,4},{14,6},{16,24},{18,... | collective-permute-start | bytes 122888 | tf_op jit(solution)/shard_map/ppermute | solution.py:111
  623.5 10.2 %collective-permute-start.4 = (bf16[1,4,5120]{2,0,1:T(2,128)(2,1)S(1)}, bf16[1,4,5120]{2,0,1:T(2,128)(2,1)S(1)}, u32[]{:S(2)}, u32[]{:S(2)}) collective-permute-start(bf16[1,4,5120]{2,0,1:T(2,128)(2,1)S(1)} %copy.212), channel_id=1, source_target_pairs={{0,10},{2,8},{4,14},{6,12},{8,2},{10,0},{12,6},{14,4},{16,26},{18,... | collective-permute-start | bytes 122888 | tf_op jit(solution)/shard_map/ppermute | solution.py:111
  626.8 8.8 %collective-permute-start.5 = (bf16[1,4,5120]{2,0,1:T(2,128)(2,1)S(1)}, bf16[1,4,5120]{2,0,1:T(2,128)(2,1)S(1)}, u32[]{:S(2)}, u32[]{:S(2)}) collective-permute-start(bf16[1,4,5120]{2,0,1:T(2,128)(2,1)S(1)} %copy.213), channel_id=1, source_target_pairs={{0,12},{2,14},{4,8},{6,10},{8,4},{10,6},{12,0},{14,2},{16,28},{18,... | collective-permute-start | bytes 122888 | tf_op jit(solution)/shard_map/ppermute | solution.py:111
  627.3 10.7 %collective-permute-start.6 = (bf16[1,4,5120]{2,0,1:T(2,128)(2,1)S(1)}, bf16[1,4,5120]{2,0,1:T(2,128)(2,1)S(1)}, u32[]{:S(2)}, u32[]{:S(2)}) collective-permute-start(bf16[1,4,5120]{2,0,1:T(2,128)(2,1)S(1)} %copy.214), channel_id=1, source_target_pairs={{0,14},{2,12},{4,10},{6,8},{8,6},{10,4},{12,2},{14,0},{16,30},{18,... | collective-permute-start | bytes 122888 | tf_op jit(solution)/shard_map/ppermute | solution.py:111
  629.9 14.8 %collective-permute-start.7 = (bf16[1,4,5120]{2,0,1:T(2,128)(2,1)S(1)}, bf16[1,4,5120]{2,0,1:T(2,128)(2,1)S(1)}, u32[]{:S(2)}, u32[]{:S(2)}) collective-permute-start(bf16[1,4,5120]{2,0,1:T(2,128)(2,1)S(1)} %copy.215), channel_id=1, source_target_pairs={{0,16},{2,18},{4,20},{6,22},{8,24},{10,26},{12,28},{14,30},{16,0},... | collective-permute-start | bytes 122888 | tf_op jit(solution)/shard_map/ppermute | solution.py:111
  631.4 16.6 %collective-permute-start.8 = (bf16[1,4,5120]{2,0,1:T(2,128)(2,1)S(1)}, bf16[1,4,5120]{2,0,1:T(2,128)(2,1)S(1)}, u32[]{:S(2)}, u32[]{:S(2)}) collective-permute-start(bf16[1,4,5120]{2,0,1:T(2,128)(2,1)S(1)} %copy.216), channel_id=1, source_target_pairs={{0,18},{2,16},{4,22},{6,20},{8,26},{10,24},{12,30},{14,28},{16,2},... | collective-permute-start | bytes 122888 | tf_op jit(solution)/shard_map/ppermute | solution.py:111
  633.7 16.1 %collective-permute-start.9 = (bf16[1,4,5120]{2,0,1:T(2,128)(2,1)S(1)}, bf16[1,4,5120]{2,0,1:T(2,128)(2,1)S(1)}, u32[]{:S(2)}, u32[]{:S(2)}) collective-permute-start(bf16[1,4,5120]{2,0,1:T(2,128)(2,1)S(1)} %copy.217), channel_id=1, source_target_pairs={{0,20},{2,22},{4,16},{6,18},{8,28},{10,30},{12,24},{14,26},{16,4},... | collective-permute-start | bytes 122888 | tf_op jit(solution)/shard_map/ppermute | solution.py:111
  635.7 26.0 %collective-permute-start.10 = (bf16[1,4,5120]{2,0,1:T(2,128)(2,1)S(1)}, bf16[1,4,5120]{2,0,1:T(2,128)(2,1)S(1)}, u32[]{:S(2)}, u32[]{:S(2)}) collective-permute-start(bf16[1,4,5120]{2,0,1:T(2,128)(2,1)S(1)} %copy.218), channel_id=1, source_target_pairs={{0,22},{2,20},{4,18},{6,16},{8,30},{10,28},{12,26},{14,24},{16,6},... | collective-permute-start | bytes 122888 | tf_op jit(solution)/shard_map/ppermute | solution.py:111
  638.0 24.4 %collective-permute-start.11 = (bf16[1,4,5120]{2,0,1:T(2,128)(2,1)S(1)}, bf16[1,4,5120]{2,0,1:T(2,128)(2,1)S(1)}, u32[]{:S(2)}, u32[]{:S(2)}) collective-permute-start(bf16[1,4,5120]{2,0,1:T(2,128)(2,1)S(1)} %copy.219), channel_id=1, source_target_pairs={{0,24},{2,26},{4,28},{6,30},{8,16},{10,18},{12,20},{14,22},{16,8},... | collective-permute-start | bytes 122888 | tf_op jit(solution)/shard_map/ppermute | solution.py:111
  644.7 18.6 %collective-permute-start.12 = (bf16[1,4,5120]{2,0,1:T(2,128)(2,1)S(1)}, bf16[1,4,5120]{2,0,1:T(2,128)(2,1)S(1)}, u32[]{:S(2)}, u32[]{:S(2)}) collective-permute-start(bf16[1,4,5120]{2,0,1:T(2,128)(2,1)S(1)} %copy.220), channel_id=1, source_target_pairs={{0,26},{2,24},{4,30},{6,28},{8,18},{10,16},{12,22},{14,20},{16,10}... | collective-permute-start | bytes 122888 | tf_op jit(solution)/shard_map/ppermute | solution.py:111
  648.0 16.2 %collective-permute-start.13 = (bf16[1,4,5120]{2,0,1:T(2,128)(2,1)S(1)}, bf16[1,4,5120]{2,0,1:T(2,128)(2,1)S(1)}, u32[]{:S(2)}, u32[]{:S(2)}) collective-permute-start(bf16[1,4,5120]{2,0,1:T(2,128)(2,1)S(1)} %copy.221), channel_id=1, source_target_pairs={{0,28},{2,30},{4,24},{6,26},{8,20},{10,22},{12,16},{14,18},{16,12}... | collective-permute-start | bytes 122888 | tf_op jit(solution)/shard_map/ppermute | solution.py:111
  649.8 15.3 %collective-permute-start.14 = (bf16[1,4,5120]{2,0,1:T(2,128)(2,1)S(1)}, bf16[1,4,5120]{2,0,1:T(2,128)(2,1)S(1)}, u32[]{:S(2)}, u32[]{:S(2)}) collective-permute-start(bf16[1,4,5120]{2,0,1:T(2,128)(2,1)S(1)} %copy.222), channel_id=1, source_target_pairs={{0,30},{2,28},{4,26},{6,24},{8,22},{10,20},{12,18},{14,16},{16,14}... | collective-permute-start | bytes 122888 | tf_op jit(solution)/shard_map/ppermute | solution.py:111
  672.8 11.9 %all-to-all-start = ((f32[16,1,4]{2,1,0:T(1,128)}), f32[16,1,4]{2,1,0:T(1,128)S(1)}, u32[]{:S(2)}, u32[]{:S(2)}) async-start(f32[16,1,4]{2,1,0:T(1,128)} %copy.193), calls=%async_computation | async-start | bytes 16384 | tf_op jit(solution)/shard_map/all_to_all | solution.py:76
  (21 other events, 77.3 us)
Sparse Core Ops, SparseCore 0:
  53.2 432.8 all-gather.4
